TPU v7x, 32 devices: a whole 2x2x4 slice. The times are simulated.
32 devices in a mesh: fsdp: 8 (over z, y), tp: 4 (over x, core).
Axes of the slice: x: 2, y: 2, z: 4, core: 2. Of those that a mesh axis runs over, the one named last changes fastest.
Arguments:
- grads: bfloat16 [8, 2, 4096, 2048], P('fsdp', None, 'tp'), may hold values from -144 to 144
- master: float32 [4096, 2048], P('tp', 'fsdp'), may hold values from -0.3125 to 0.3125
- moment: float32 [4096, 2048], P('tp', 'fsdp'), may hold values from -1.5 to 1.5
- second: float32 [4096, 2048], P('tp', 'fsdp'), may hold values from 0.02 to 0.3
- stats: float32 [4, 1024, 1024], P('tp', 'fsdp'), may hold values from -0.05 to 0.35
- basis: float32 [4, 1024, 1024], P('tp', 'fsdp'), may hold values from -0.5 to 1.5
Outputs:
- weights: bfloat16 [4096, 2048], P('tp')
- master_new: float32 [4096, 2048], P('tp', 'fsdp')
- moment_new: float32 [4096, 2048], P('tp', 'fsdp')
- second_new: float32 [4096, 2048], P('tp', 'fsdp')
- stats_new: float32 [4, 1024, 1024], P('tp', 'fsdp')
- basis_new: float32 [4, 1024, 1024], P('tp', 'fsdp')
All inputs are finite; a program needn't handle non-finite values.
Results may differ from a plain program's by a relative error of at most 0.007.
Values may be sent and summed in bfloat16 or wider, within the bound.
A program may use at most 128 MiB of HBM per device.

v0:
```python
import jax
import jax.numpy as jnp
from jax import lax
from jax.sharding import PartitionSpec as P

D = 4096
KVW = 2048
NSK = 2


poly_first = 3.4445
poly_second = -4.775
poly_third = 2.0315


def gram_of(current):
    local_gram = jnp.dot(current.T, current, precision=lax.Precision.HIGHEST)
    return lax.psum(local_gram.astype(jnp.bfloat16), "fsdp").astype(jnp.float32)


def body(grads, master, moment, second, stats, basis):
    high = lax.Precision.HIGHEST
    local = jnp.sum(grads.astype(jnp.float32), axis=(0, 1))
    summed = lax.psum_scatter(local, "fsdp", scatter_dimension=1, tiled=True)
    squares = lax.psum(jnp.sum(summed * summed), ("fsdp", "tp"))
    clipped = summed * jnp.minimum(1.0, jnp.sqrt(float(D * KVW) / (squares + 1e-06)))
    own_rows = basis[0]
    stat_rows = stats[0]
    whole = lax.all_gather(own_rows, "fsdp", axis=0, tiled=True)
    rotated = jnp.dot(whole.T, clipped, precision=high)
    moment_new = 0.9 * moment + 0.1 * rotated
    second_new = 0.95 * second + 0.05 * rotated * rotated
    update = moment_new / (jnp.sqrt(second_new) + 1e-08)
    delta = jnp.dot(whole, update, precision=high)
    master_new = master - 0.01 * (delta + 0.1 * master)
    weights = lax.all_gather(master_new.astype(jnp.bfloat16), "fsdp", axis=1, tiled=True)
    outer = lax.psum_scatter(
        jnp.dot(clipped, clipped.T, precision=high).astype(jnp.bfloat16),
        "fsdp",
        scatter_dimension=0,
        tiled=True,
    ).astype(jnp.float32)
    stats_new = 0.9 * stat_rows + 0.1 / KVW * outer
    power = jnp.dot(stats_new, whole, precision=high)
    total_sq = lax.psum(jnp.sum(power * power), "fsdp")
    current = power / jnp.sqrt(total_sq + 1e-06)
    first_gram = gram_of(current)
    for step in range(NSK):
        gram = first_gram if step == 0 else gram_of(current)
        product = jnp.dot(current, gram, precision=high)
        second_term = jnp.dot(product, gram, precision=high)
        current = poly_first * current + poly_second * product + poly_third * second_term
    return (weights, master_new, moment_new, second_new, stats_new[None], current[None])


def solution(mesh):
    in_specs = (
        P("fsdp", None, "tp", None),
        P("tp", "fsdp"),
        P("tp", "fsdp"),
        P("tp", "fsdp"),
        P("tp", "fsdp", None),
        P("tp", "fsdp", None),
    )
    out_specs = (
        P("tp", None),
        P("tp", "fsdp"),
        P("tp", "fsdp"),
        P("tp", "fsdp"),
        P("tp", "fsdp", None),
        P("tp", "fsdp", None),
    )
    return jax.shard_map(body, mesh=mesh, in_specs=in_specs, out_specs=out_specs, check_vma=False)
```

profile of v0, /device:TPU:28, one launch (start us, length us, event | category | flops | bytes accessed | tf_op | source)
XLA Modules:
  0.0 634.1 jit_solution(12777365153382909776)
XLA Ops:
  7.2 0.0 reduce-scatter.3.cloned.1.call-start
  7.2 9.6 %convert_reduce_fusion = f32[1024,2048]{1,0:T(8,128)} fusion(bf16[1,2,1024,2048]{3,2,1,0:T(8,128)(2,1)} %param.6), kind=kLoop, calls=%fused_computation | loop fusion | flops 6291456 | bytes 16777216 | tf_op jit(solution)/shard_map/reduce_sum | solution.py:23
  16.8 0.0 reduce-scatter.3.cloned.1.call-update
  16.8 0.0 copy-start.4
  16.8 0.0 all-gather.6.cloned.1.call-start
  16.9 0.7 all-gather.6.cloned.1.call-update
  17.6 0.0 reduce-scatter.5.cloned.1.call-start
  17.6 147.8 %reduce-scatter.3.cloned.1.call-done = f32[1024,256]{1,0:T(8,128)} async-done(((f32[1024,2048]{1,0:T(8,128)}), f32[1024,256]{1,0:T(8,128)}) %reduce-scatter.3.cloned.1.call-update) | async-done | bytes 1048592 | tf_op jit(solution)/shard_map/reduce_scatter | solution.py:24
  165.4 2.1 multiply_reduce_fusion
  167.5 42.2 %psum.28 = f32[]{:T(128)} all-reduce(f32[]{:T(128)} %multiply_reduce_fusion), channel_id=1, replica_groups=mesh['fsdp'=8,'tp'=4] {'fsdp','tp'}, use_global_device_ids=true, to_apply=%region_3.0 | all-reduce | flops 1 | bytes 8 | tf_op jit(solution)/shard_map/psum | solution.py:25
  210.4 6.4 %convolution_convert_fusion.2 = bf16[1024,1024]{1,0:T(8,128)(2,1)} fusion(f32[1024,256]{1,0:T(8,128)} %reduce-scatter.3.cloned.1.call-done, f32[]{:T(128)S(6)} %min_shard_map.3), kind=kOutput, calls=%fused_computation.9 | convolution fusion | flops 3222536192 | bytes 3145732 | tf_op jit(solution)/shard_map/dot_general | solution.py:38
  216.9 0.0 reduce-scatter.5.cloned.1.call-update
  216.9 0.0 copy-start.9
  216.9 0.0 all-reduce.3.cloned.1.call-start
  217.0 24.0 %all-gather.6.cloned.1.call-done = f32[1,1024,1024]{2,1,0:T(8,128)} async-done(((f32[1,128,1024]{2,1,0:T(8,128)}), f32[1,1024,1024]{2,1,0:T(8,128)}) %all-gather.6.cloned.1.call-update) | async-done | bytes 4194320 | tf_op jit(solution)/shard_map/all_gather | solution.py:29
  240.9 70.9 %reduce-scatter.5.cloned.1.call-done = bf16[128,1024]{1,0:T(8,128)(2,1)} async-done(((bf16[1024,1024]{1,0:T(8,128)(2,1)}), bf16[128,1024]{1,0:T(8,128)(2,1)}) %reduce-scatter.5.cloned.1.call-update) | async-done | bytes 262160 | tf_op jit(solution)/shard_map/reduce_scatter | solution.py:37
  311.8 0.0 copy-done.4
  311.8 5.3 multiply_reduce_fusion.1
  317.2 17.9 %psum.29 = f32[]{:T(128)} all-reduce(f32[]{:T(128)} %get-tuple-element.22), channel_id=1, replica_groups=mesh['fsdp'=8,'tp'=4] {'fsdp'}, use_global_device_ids=true, to_apply=%region_6.0 | all-reduce | flops 1 | bytes 8 | tf_op jit(solution)/shard_map/psum | solution.py:45
  335.8 4.7 convolution_convert_fusion.1
  340.5 0.0 all-reduce.3.cloned.1.call-update
  340.5 0.0 all-gather.4.cloned.1.call-start
  340.6 0.0 copy-done.9
  340.6 1.3 copy.20
  341.9 2.5 copy.21
  344.4 0.0 copy-done.6
  344.4 2.5 copy.23
  347.0 0.0 copy-done.1
  347.0 7.1 %fusion.24 = (f32[1024,256]{0,1:T(8,128)S(1)}, f32[1024,256]{0,1:T(8,128)S(1)}) fusion(f32[1024,256]{0,1:T(8,128)} %copy.21, f32[1024,256]{0,1:T(8,128)} %copy.20, f32[1,1024,1024]{2,1,0:T(8,128)} %all-gather.6.cloned.1.call-done, f32[1024,256]{1,0:T(8,128)S(1)} %copy-done.1, f32[]{:T(128)S(6)} %min_shard_map.3), kind=kOutput, calls=%fused_computation.21 | convolution fusion | flops 3223322624 | bytes 9437188 | tf_op jit(solution)/shard_map/dot_general | solution.py:30
  354.1 0.0 copy-start.7
  354.1 5.3 fusion.40
  359.4 0.0 all-gather.4.cloned.1.call-update
  359.4 0.3 all-reduce.5.cloned.1.call-start
  359.7 83.0 %all-reduce.3.cloned.1.call-done = bf16[1024,1024]{1,0:T(8,128)(2,1)} async-done(((bf16[1024,1024]{1,0:T(8,128)(2,1)}), bf16[1024,1024]{1,0:T(8,128)(2,1)}) %all-reduce.3.cloned.1.call-update) | async-done | bytes 2097168 | tf_op jit(solution)/shard_map/psum | solution.py:18
  442.7 2.6 fusion.39
  445.3 2.7 fusion.23
  447.9 4.7 convolution_convert_fusion
  452.7 0.0 all-reduce.5.cloned.1.call-update
  452.7 1.3 copy.26
  454.0 1.3 copy.27
  455.3 2.7 copy.25
  458.0 0.0 copy-done.5
  458.0 0.9 fusion.33
  458.8 58.4 %all-gather.4.cloned.1.call-done = bf16[1024,2048]{0,1:T(8,128)(2,1)} async-done(((bf16[1024,256]{0,1:T(8,128)(2,1)}), bf16[1024,2048]{0,1:T(8,128)(2,1)}) %all-gather.4.cloned.1.call-update) | async-done | bytes 4194320 | tf_op jit(solution)/shard_map/all_gather | solution.py:36
  517.2 6.4 %copy.24 = bf16[1024,2048]{1,0:T(8,128)(2,1)} copy(bf16[1024,2048]{0,1:T(8,128)(2,1)} %all-gather.4.cloned.1.call-done) | data formatting | bytes 8388608
  523.7 98.9 %all-reduce.5.cloned.1.call-done = bf16[1024,1024]{1,0:T(8,128)(2,1)} async-done(((bf16[1024,1024]{1,0:T(8,128)(2,1)}), bf16[1024,1024]{1,0:T(8,128)(2,1)}) %all-reduce.5.cloned.1.call-update) | async-done | bytes 2097168 | tf_op jit(solution)/shard_map/psum | solution.py:18
  622.6 2.8 fusion.41
  625.4 1.9 fusion.22
  (12 shorter events, 0.0 us)
Async XLA Ops:
  7.2 158.2 %reduce-scatter.3.cloned.1.call-start = ((), (), s32[]{:S(2)}) async-start(), calls=%async_computation.2 | async-start | bytes 9437184 | tf_op jit(solution)/shard_map/reduce_scatter | solution.py:24
  16.8 295.0 %copy-start.4 = (f32[1,128,1024]{2,1,0:T(8,128)S(1)}, f32[1,128,1024]{2,1,0:T(8,128)}, u32[]{:S(2)}) copy-start(f32[1,128,1024]{2,1,0:T(8,128)} %param.10) | copy-start | bytes 1572868
  16.8 224.1 %all-gather.6.cloned.1.call-start = ((), (), s32[]{:S(2)}) async-start(), calls=%async_computation.7 | async-start | bytes 4718592 | tf_op jit(solution)/shard_map/all_gather | solution.py:29
  17.6 294.2 %reduce-scatter.5.cloned.1.call-start = ((), (), s32[]{:S(2)}) async-start(), calls=%async_computation.4 | async-start | bytes 2359296 | tf_op jit(solution)/shard_map/reduce_scatter | solution.py:37
  216.9 123.7 %copy-start.9 = (f32[1024,256]{1,0:T(8,128)S(1)}, f32[1024,256]{1,0:T(8,128)}, u32[]{:S(2)}) copy-start(f32[1024,256]{1,0:T(8,128)} %param.8) | copy-start | bytes 3145732
  216.9 225.8 %all-reduce.3.cloned.1.call-start = ((), (), s32[]{:S(2)}) async-start(), calls=%async_computation.5 | async-start | bytes 4194304 | tf_op jit(solution)/shard_map/psum | solution.py:18
  317.2 27.3 %copy-start.6 = (f32[128,1024]{1,0:T(8,128)}, f32[128,1024]{1,0:T(8,128)S(1)}, u32[]{:S(2)}) copy-start(f32[128,1024]{1,0:T(8,128)S(1)} %get-tuple-element.23) | copy-start | bytes 1572868
  340.5 6.5 %copy-start.1 = (f32[1024,256]{1,0:T(8,128)S(1)}, f32[1024,256]{1,0:T(8,128)}, u32[]{:S(2)}) copy-start(f32[1024,256]{1,0:T(8,128)} %reduce-scatter.3.cloned.1.call-done) | copy-start | bytes 3145732
  340.5 176.7 %all-gather.4.cloned.1.call-start = ((), (), s32[]{:S(2)}) async-start(), calls=%async_computation.3 | async-start | bytes 4718592 | tf_op jit(solution)/shard_map/all_gather | solution.py:36
  347.0 7.1 %copy-start = (f32[1,1024,1024]{2,1,0:T(8,128)S(1)}, f32[1,1024,1024]{2,1,0:T(8,128)}, u32[]{:S(2)}) copy-start(f32[1,1024,1024]{2,1,0:T(8,128)} %all-gather.6.cloned.1.call-done) | copy-start | bytes 12582916
  347.0 7.1 %copy-start.3 = (f32[1024,256]{0,1:T(8,128)S(1)}, f32[1024,256]{0,1:T(8,128)}, u32[]{:S(2)}) copy-start(f32[1024,256]{0,1:T(8,128)} %copy.23) | copy-start | bytes 3145732
  354.1 88.6 %copy-start.7 = (f32[128,1024]{1,0:T(8,128)S(1)}, f32[128,1024]{1,0:T(8,128)}, u32[]{:S(2)}) copy-start(f32[128,1024]{1,0:T(8,128)} %copy-done.6) | copy-start | bytes 1572868
  359.4 263.2 %all-reduce.5.cloned.1.call-start = ((), (), s32[]{:S(2)}) async-start(), calls=%async_computation.6 | async-start | bytes 4194304 | tf_op jit(solution)/shard_map/psum | solution.py:18
  452.7 5.3 copy-start.5
  452.7 5.3 copy-start.8
  622.6 2.8 copy-start.2
Sparse Core Ops, SparseCore 0:
  16.9 148.4 reduce-scatter.2
  167.8 73.1 all-gather.5
  245.4 66.3 reduce-scatter.4
  340.6 101.9 all-reduce.2
  445.4 71.7 all-gather.3
  521.2 101.3 all-reduce.4
where the time goes:
time: 638 us; the launch traced here: 634 us
  waiting for transfers between devices  484 us (76%)
  blocking collectives  60.1 us (9%)
  matrix products  43.4 us (7%)
  local copies, waits for them, and re-layouts  18.1 us (3%)
  between operations  15.6 us (2%)
  other arithmetic  12.6 us (2%)
    psum x2, waiting for transfers between devices, gram_of(): return lax.psum(local_gram.astype(jnp.bfloat16), 'fsdp').astype(jnp.float32)  182 us
    reduce_scatter x1, waiting for transfers between devices, body(): summed = lax.psum_scatter(local, 'fsdp', scatter_dimension=1, tiled=True)  148 us
    reduce_scatter x1, waiting for transfers between devices, body(): lax.psum_scatter(jnp.dot(clipped, clipped.T, precision=high).astype(jnp.b...  70.9 us
    all_gather x1, waiting for transfers between devices, body(): lax.all_gather(master_new.astype(jnp.bfloat16), 'fsdp', axis=1, tiled=True)  58.4 us
    psum x1, blocking collectives, body(): squares = lax.psum(jnp.sum(summed * summed), ('fsdp', 'tp'))  42.2 us
    all_gather x1, waiting for transfers between devices, body(): whole = lax.all_gather(own_rows, 'fsdp', axis=0, tiled=True)  24 us
    unnamed x27, local copies, waits for them, and re-layouts  18.1 us
    psum x1, blocking collectives, body(): total_sq = lax.psum(jnp.sum(power * power), 'fsdp')  17.9 us
  transfers between devices with their start and end apart: 6, of which 6 were waited for; matrix products, arithmetic and copies ran while one was open for 8% of the time, Pallas kernels for 0%

commit v1 on v0

v1 whole, which is shorter than its diff:
```python
import jax
import jax.numpy as jnp
from jax import lax
from jax.sharding import PartitionSpec as P

D = 4096
KVW = 2048

poly_first = 3.4445
poly_second = -4.775
poly_third = 2.0315
bf16 = jnp.bfloat16
f32 = jnp.float32


def exact(a, b):
    return jnp.dot(a, b, precision=lax.Precision.HIGHEST)


def split(a):
    top = a.astype(bf16)
    return top, (a - top.astype(f32)).astype(bf16)


def three(a, b):
    a_top, a_low = split(a)
    b_top, b_low = split(b)
    mm = lambda u, v: jnp.dot(u, v, preferred_element_type=f32)
    return mm(a_top, b_top) + (mm(a_low, b_top) + mm(a_top, b_low))


def body(grads, master, moment, second, stats, basis):
    n = lax.axis_size("fsdp")
    rows = master.shape[0]
    cols = master.shape[1]
    own_rows = basis[0]
    stat_rows = stats[0]
    whole = lax.all_gather(own_rows.astype(bf16), "fsdp", axis=0, tiled=True)
    local = jnp.sum(grads.astype(f32), axis=(0, 1)).astype(bf16)
    pieces = lax.all_to_all(local, "fsdp", split_axis=1, concat_axis=0, tiled=True)
    summed = jnp.sum(pieces.reshape(n, rows, cols).astype(f32), axis=0)
    squares = jnp.sum(lax.all_gather(jnp.sum(summed * summed).reshape(1), ("fsdp", "tp")))
    ratio = jnp.minimum(1.0, jnp.sqrt(float(D * KVW) / (squares + 1e-06)))
    total = summed.astype(bf16)
    part = jnp.dot(total, total.T, preferred_element_type=f32).astype(bf16)
    strips = lax.all_to_all(part, "fsdp", split_axis=0, concat_axis=0, tiled=True)
    outer = jnp.sum(strips.reshape(n, rows // n, rows).astype(f32), axis=0) * (ratio * ratio)
    stats_new = 0.9 * stat_rows + 0.1 / KVW * outer
    s_top, s_low = split(stats_new)
    power = jnp.dot(s_top, whole, preferred_element_type=f32) + jnp.dot(s_low, whole, preferred_element_type=f32)
    every = lax.all_gather(power.astype(bf16), "fsdp", axis=0, tiled=True)
    rotated = jnp.dot(whole.T, total, preferred_element_type=f32) * ratio
    moment_new = 0.9 * moment + 0.1 * rotated
    second_new = 0.95 * second + 0.05 * rotated * rotated
    update = moment_new / (jnp.sqrt(second_new) + 1e-08)
    delta = jnp.dot(whole, update.astype(bf16), preferred_element_type=f32)
    master_new = master - 0.01 * (delta + 0.1 * master)
    weights = lax.all_gather(master_new.astype(bf16), "fsdp", axis=1, tiled=True)
    raw = jnp.dot(every.T, every, preferred_element_type=f32)
    diag = lax.broadcasted_iota(jnp.int32, (rows, rows), 0) == lax.broadcasted_iota(jnp.int32, (rows, rows), 1)
    norm = 1.0 / jnp.sqrt(jnp.sum(jnp.where(diag, raw, 0.0)) + 1e-06)
    gram = raw * (norm * norm)
    current = power * norm
    mixed = jnp.where(diag, poly_first, 0.0) + poly_second * gram + poly_third * three(gram, gram)
    current = three(current, mixed)
    gram = three(mixed, three(mixed, gram))
    product = three(current, gram)
    current = poly_first * current + poly_second * product + poly_third * three(product, gram)
    return (weights, master_new, moment_new, second_new, stats_new[None], current[None])


def solution(mesh):
    in_specs = (
        P("fsdp", None, "tp", None),
        P("tp", "fsdp"),
        P("tp", "fsdp"),
        P("tp", "fsdp"),
        P("tp", "fsdp", None),
        P("tp", "fsdp", None),
    )
    out_specs = (
        P("tp", None),
        P("tp", "fsdp"),
        P("tp", "fsdp"),
        P("tp", "fsdp"),
        P("tp", "fsdp", None),
        P("tp", "fsdp", None),
    )
    return jax.shard_map(body, mesh=mesh, in_specs=in_specs, out_specs=out_specs, check_vma=False)
```

time: 638 us -> 367 us (0.58)
  waiting for transfers between devices: 484 us -> 60.6 us
  blocking collectives: 60.1 us -> 180 us
  local copies, waits for them, and re-layouts: 18.1 us -> 34.4 us
    reduce_scatter x2 -> x0, waiting for transfers between devices: 219 us -> none  [the longest x1 148 us: body(): summed = lax.psum_scatter(local, 'fsdp', scatter_dimension=1, tiled=True)]
    psum x2 -> x0, waiting for transfers between devices: 182 us -> none  [gram_of(): return lax.psum(local_gram.astype(jnp.bfloat16), 'fsdp').astype(jnp.float32)]
    all_to_all x0 -> x1, blocking collectives: none -> 96.8 us  [body(): lax.all_to_all(local, 'fsdp', split_axis=1, concat_axis=0, tiled=True)]
    unnamed x0 -> x1, blocking collectives: none -> 82.9 us
    psum x2 -> x0, blocking collectives: 60.1 us -> none  [the longest x1 42.2 us: body(): squares = lax.psum(jnp.sum(summed * summed), ('fsdp', 'tp'))]
    all_gather x2 -> x3, waiting for transfers between devices: 82.4 us -> 60.5 us  [the longest x1 35.5 us: body(): lax.all_gather(master_new.astype(bf16), 'fsdp', axis=1, tiled=True)]
    all_to_all x0 -> x1, local copies, waits for them, and re-layouts: none -> 6.42 us  [body(): lax.all_to_all(local, 'fsdp', split_axis=1, concat_axis=0, tiled=True)]
    reduce_sum x0 -> x1, local copies, waits for them, and re-layouts: none -> 6.39 us  [body(): local = jnp.sum(grads.astype(f32), axis=(0, 1)).astype(bf16)]
  transfers between devices with their start and end apart: 6 -> 4, of which waited for: 6 -> 2; matrix products, arithmetic and copies ran while one was open for 8% -> 18% of each run, Pallas kernels for 0% -> 0%
where the time goes in v1:
time: 367 us; the launch traced here: 362 us
  blocking collectives  180 us (49%)
  waiting for transfers between devices  60.6 us (17%)
  matrix products  47.8 us (13%)
  local copies, waits for them, and re-layouts  34.4 us (9%)
  other arithmetic  17.7 us (5%)
  between operations  15.4 us (4%)
  starting transfers between devices  6.26 us (2%)
    all_to_all x1, blocking collectives, body(): lax.all_to_all(local, 'fsdp', split_axis=1, concat_axis=0, tiled=True)  96.8 us
    unnamed x1, blocking collectives  82.9 us
    all_gather x1, waiting for transfers between devices, body(): lax.all_gather(master_new.astype(bf16), 'fsdp', axis=1, tiled=True)  35.5 us
    dot_general x18, matrix products, three(): mm = lambda u, v: jnp.dot(u, v, preferred_element_type=f32)  27.2 us
    all_gather x1, waiting for transfers between devices, body(): every = lax.all_gather(power.astype(bf16), 'fsdp', axis=0, tiled=True)  25 us
    unnamed x25, local copies, waits for them, and re-layouts  21.6 us
    reduce_sum x1, other arithmetic, body(): local = jnp.sum(grads.astype(f32), axis=(0, 1)).astype(bf16)  8.78 us
  transfers between devices with their start and end apart: 4, of which 2 were waited for; matrix products, arithmetic and copies ran while one was open for 18% of the time, Pallas kernels for 0%

profile of v1, /device:TPU:28, one launch (start us, length us, event | category | flops | bytes accessed | tf_op | source)
XLA Modules:
  0.0 361.8 jit_solution(5923313504358977901)
XLA Ops:
  7.2 8.8 %reduce_sum.57 = bf16[1024,2048]{1,0:T(8,128)(2,1)} reduce(bf16[1,2,1024,2048]{3,2,1,0:T(8,128)(2,1)} %param.6, bf16[]{:T(256)} %constant.16.clone.1), dimensions={0,1}, to_apply=%region_0.0 | reduce | flops 2097152 | bytes 12582914 | tf_op jit(solution)/shard_map/reduce_sum | solution.py:39
  16.0 6.4 %copy.48 = bf16[1024,2048]{0,1:T(8,128)(2,1)} copy(bf16[1024,2048]{1,0:T(8,128)(2,1)} %reduce_sum.57) | data formatting | bytes 8388608 | tf_op jit(solution)/shard_map/reduce_sum | solution.py:39
  22.3 6.4 %copy.49 = bf16[1024,8,256]{2,0,1:T(8,128)(2,1)} copy(bf16[1024,8,256]{0,2,1:T(8,128)(2,1)} %bitcast.79) | data formatting | bytes 8388608 | tf_op jit(solution)/shard_map/all_to_all | solution.py:40
  28.8 96.8 %all_to_all.22 = bf16[1024,8,256]{2,0,1:T(8,128)(2,1)S(1)} all-to-all(bf16[1024,8,256]{2,0,1:T(8,128)(2,1)} %copy.49), channel_id=1, replica_groups=mesh['fsdp'=8,'tp'=4] {'fsdp'}, dimensions={1} | all-to-all | bytes 8388608 | tf_op jit(solution)/shard_map/all_to_all | solution.py:40
  125.5 0.6 convert_reduce_fusion
  126.1 2.1 convolution_convert_fusion
  128.2 6.0 %all-to-all-start.1 = ((bf16[8,128,1024]{2,1,0:T(8,128)(2,1)}), bf16[8,128,1024]{2,1,0:T(8,128)(2,1)S(1)}, u32[]{:S(2)}, u32[]{:S(2)}) async-start(bf16[8,128,1024]{2,1,0:T(8,128)(2,1)} %bitcast.80), calls=%async_computation.1 | async-start | bytes 4194304 | tf_op jit(solution)/shard_map/all_to_all | solution.py:46
  134.2 1.8 convert_element_type.119
  136.0 0.9 multiply_reduce_fusion
  136.9 0.8 dynamic-update-slice
  137.7 82.9 %all-reduce = f32[32]{0:T(128)S(1)} all-reduce(f32[32]{0:T(128)S(1)} %dynamic-update-slice), channel_id=1, replica_groups=mesh['fsdp'=8,'tp'=4] {'fsdp','tp'}, use_global_device_ids=true, to_apply=%add | all-reduce | flops 32 | bytes 256
  220.5 0.6 reduce.2
  221.9 1.1 convert_reduce_fusion.1
  223.0 2.5 fusion.1
  225.8 1.4 fusion.72
  227.2 0.2 all-gather.5.cloned.1.call-start
  227.5 2.5 copy.47
  230.0 2.5 copy.50
  232.5 2.5 copy.52
  235.1 3.8 %fusion.36 = (f32[1024,256]{0,1:T(8,128)}, f32[1024,256]{0,1:T(8,128)}) fusion(f32[1024,256]{0,1:T(8,128)} %copy.50, f32[1024,256]{0,1:T(8,128)} %copy.47, f32[]{:T(128)S(6)} %min.3, bf16[1,1024,1024]{2,1,0:T(8,128)(2,1)S(1)} %copy-done, f32[1024,256]{1,0:T(8,128)S(1)} %convert_reduce_fusion), kind=kOutput, calls=%fused_computation.39 | convolution fusion | flops 539230208 | bytes 7340036 | tf_op jit(solution)/shard_map/dot_general | solution.py:52
  238.9 2.6 copy.55
  241.5 1.3 copy.56
  242.8 3.6 fusion.71
  246.5 2.6 copy.54
  249.1 0.9 bitcast_add_fusion.1
  250.0 25.0 %all-gather.7.cloned.1.call-done = bf16[1024,1024]{1,0:T(8,128)(2,1)} async-done(((bf16[128,1024]{1,0:T(8,128)(2,1)}), bf16[1024,1024]{1,0:T(8,128)(2,1)}) %all-gather.7.cloned.1.call-update) | async-done | bytes 2097168 | tf_op jit(solution)/shard_map/all_gather | solution.py:51
  275.0 7.2 %select_reduce_fusion = (f32[]{:T(128)}, f32[1024,1024]{1,0:T(8,128)}) fusion(bf16[1024,1024]{1,0:T(8,128)(2,1)} %all-gather.7.cloned.1.call-done), kind=kOutput, calls=%fused_computation.8 | convolution fusion | flops 2150629376 | bytes 6291460 | tf_op jit(solution)/shard_map/dot_general | solution.py:59
  282.9 3.1 subtract_convert_fusion.3
  286.0 2.3 fusion.73
  288.3 2.3 fusion.74
  290.7 3.2 subtract_convert_fusion.2
  293.9 0.4 fusion.38
  294.4 0.4 fusion.44
  294.8 0.5 fusion.35
  295.3 2.3 fusion.76
  297.6 2.3 fusion.75
  300.0 2.6 add_add_fusion.1
  302.5 2.3 fusion.54
  304.9 2.3 fusion
  307.2 2.4 add_add_fusion
  309.6 0.4 fusion.39
  310.0 0.4 fusion.58
  310.5 0.5 fusion.34
  311.0 0.5 fusion.40
  311.4 0.5 fusion.50
  311.9 1.4 fusion.33
  313.3 35.5 %all-gather.5.cloned.1.call-done = bf16[1024,2048]{0,1:T(8,128)(2,1)} async-done(((bf16[1024,256]{0,1:T(8,128)(2,1)}), bf16[1024,2048]{0,1:T(8,128)(2,1)}) %all-gather.5.cloned.1.call-update) | async-done | bytes 4194320 | tf_op jit(solution)/shard_map/all_gather | solution.py:58
  348.8 6.4 %copy.53 = bf16[1024,2048]{1,0:T(8,128)(2,1)} copy(bf16[1024,2048]{0,1:T(8,128)(2,1)} %all-gather.5.cloned.1.call-done) | data formatting | bytes 8388608
  (24 shorter events, 0.3 us)
Async XLA Ops:
  128.2 93.7 %all-to-all-start.1 = ((bf16[8,128,1024]{2,1,0:T(8,128)(2,1)}), bf16[8,128,1024]{2,1,0:T(8,128)(2,1)S(1)}, u32[]{:S(2)}, u32[]{:S(2)}) async-start(bf16[8,128,1024]{2,1,0:T(8,128)(2,1)} %bitcast.80), calls=%async_computation.1 | async-start | bytes 4194304 | tf_op jit(solution)/shard_map/all_to_all | solution.py:46
  134.2 88.9 %all-gather.9.cloned.1.call-start = ((), (), s32[]{:S(2)}) async-start(), calls=%async_computation.4 | async-start | bytes 2359296 | tf_op jit(solution)/shard_map/all_gather | solution.py:38
  136.0 139.0 %all-gather.7.cloned.1.call-start = ((), (), s32[]{:S(2)}) async-start(), calls=%async_computation.3 | async-start | bytes 2359296 | tf_op jit(solution)/shard_map/all_gather | solution.py:51
  223.0 2.5 copy-start
  223.0 2.6 copy-start.1
  223.0 2.8 copy-start.4
  227.2 121.6 %all-gather.5.cloned.1.call-start = ((), (), s32[]{:S(2)}) async-start(), calls=%async_computation.2 | async-start | bytes 4718592 | tf_op jit(solution)/shard_map/all_gather | solution.py:58
  238.9 2.6 copy-start.7
  246.5 2.6 copy-start.2
  246.5 2.7 copy-start.5
  288.3 2.4 copy-start.6
  290.7 3.2 copy-start.3
Sparse Core Ops, SparseCore 0:
  137.7 68.6 all-gather.8
  227.4 47.5 all-gather.6
  277.1 71.6 all-gather.4

commit v2 on v0

v2 whole, which is shorter than its diff:
```python
import functools

import jax
import jax.numpy as jnp
from jax import lax
from jax.experimental import pallas as pl
from jax.experimental.pallas import tpu as pltpu
from jax.sharding import PartitionSpec as P

D = 4096
KVW = 2048

poly_first = 3.4445
poly_second = -4.775
poly_third = 2.0315
bf16 = jnp.bfloat16
f32 = jnp.float32
MESH = pl.DeviceIdType.MESH
VMEM_BYTES = 40 * 1024 * 1024


def mm(a, b):
    return jnp.dot(a.astype(bf16), b.astype(bf16), preferred_element_type=f32)


def greet(n, tp_peers):
    me = lax.axis_index("fsdp")
    barrier = pltpu.get_barrier_semaphore()
    for step in range(1, n):
        pl.semaphore_signal(barrier, inc=1, device_id={"fsdp": lax.rem(me + step, n)}, device_id_type=MESH)
    if tp_peers > 1:
        lane = lax.axis_index("tp")
        for step in range(1, tp_peers):
            pl.semaphore_signal(barrier, inc=1, device_id={"tp": lax.rem(lane + step, tp_peers)}, device_id_type=MESH)
    pl.semaphore_wait(barrier, n - 1 + tp_peers - 1)


def remote(src, dst, send_sem, recv_sem, target, axis="fsdp"):
    return pltpu.make_async_remote_copy(
        src_ref=src, dst_ref=dst, send_sem=send_sem, recv_sem=recv_sem,
        device_id={axis: target}, device_id_type=MESH,
    )


def exchange(n, produce, finish, out1, in1, out2, in2, s1, r1, s2, r2):
    half = n // 2
    me = lax.axis_index("fsdp")
    side = lax.rem(me, 2)
    pair = me // 2
    mate = me + 1 - 2 * side
    groups = [lax.rem(pair + 1 + k, half) for k in range(half)]
    first = [remote(out1.at[k], in1.at[k], s1.at[k], r1.at[k], mate) for k in range(half)]
    second = [remote(out2.at[k], in2.at[k], s2.at[k], r2.at[k], 2 * groups[k] + side) for k in range(half - 1)]

    def start(k):
        produce(2 * groups[k] + 1 - side, 2 * k, None, out1.at[k])
        first[k].start()

    for k in range(min(2, half)):
        start(k)
    for k in range(half):
        first[k].wait_recv()
        if k + 2 < half:
            start(k + 2)
        if k < half - 1:
            produce(2 * groups[k] + side, 2 * k + 1, in1.at[k], out2.at[k])
            second[k].start()
    for k in range(half - 1):
        second[k].wait_recv()
    finish(me, 2 * half - 1, in1.at[half - 1], in2)
    for k in range(half):
        first[k].wait_send()
    for k in range(half - 1):
        second[k].wait_send()


def grads_kernel(n, lanes, grads, total, squares, held, out1, in1, out2, in2, own_sq, in_sq, lane_sq, in_lane,
                 loads, s1, r1, s2, r2, sq_s, sq_r, lane_s, lane_r):
    half = n // 2
    rows, cols = total.shape
    micro = held.shape[1]
    tile = 128
    me = lax.axis_index("fsdp")
    side = lax.rem(me, 2)
    pair = me // 2
    copies = []
    for k in range(half):
        group = lax.rem(pair + 1 + k, half)
        for which, chunk in ((0, 2 * group + 1 - side), (1, 2 * group + side)):
            start = pl.multiple_of(chunk * cols, 128)
            copies.append(pltpu.make_async_copy(
                grads.at[0, :, :, pl.ds(start, cols)], held.at[2 * k + which], loads.at[2 * k + which]))
    order = [0, 2] if half > 1 else [0]
    order += [i for i in range(n) if i not in order]
    for i in order:
        copies[i].start()
    greet(n, lanes)

    def local(slot, at):
        value = held[slot, 0, at, :].astype(f32)
        for index in range(1, micro):
            value = value + held[slot, index, at, :].astype(f32)
        return value

    def produce(chunk, slot, add, out):
        copies[slot].wait()

        def step(i, carry):
            at = pl.ds(pl.multiple_of(i * tile, tile), tile)
            value = local(slot, at)
            if add is not None:
                value = value + add[at, :].astype(f32)
            out[at, :] = value.astype(bf16)
            return carry

        lax.fori_loop(0, rows // tile, step, 0)

    def finish(chunk, slot, add, others):
        copies[slot].wait()

        def step(i, carry):
            at = pl.ds(pl.multiple_of(i * tile, tile), tile)
            value = local(slot, at) + add[at, :].astype(f32)
            for k in range(half - 1):
                value = value + others[k, at, :].astype(f32)
            total[at, :] = value.astype(bf16)
            return carry + jnp.sum((value * value).reshape(tile // 8, 8, cols), axis=0)

        sums = lax.fori_loop(0, rows // tile, step, jnp.zeros((8, cols), f32))
        part = sums[:, :128]
        for c in range(1, cols // 128):
            part = part + sums[:, c * 128 : (c + 1) * 128]
        own_sq[...] = part

    exchange(n, produce, finish, out1, in1, out2, in2, s1, r1, s2, r2)
    sends = [remote(own_sq, in_sq.at[k], sq_s.at[k], sq_r.at[k], lax.rem(me + 1 + k, n)) for k in range(n - 1)]
    for send in sends:
        send.start()
    value = own_sq[...]
    for k, send in enumerate(sends):
        send.wait()
        value = value + in_sq[k]
    lane_sq[...] = value
    lane = lax.axis_index("tp")
    sends = [remote(lane_sq, in_lane.at[k], lane_s.at[k], lane_r.at[k], lax.rem(lane + 1 + k, lanes), "tp")
             for k in range(lanes - 1)]
    for send in sends:
        send.start()
    for k, send in enumerate(sends):
        send.wait()
        value = value + in_lane[k]
    squares[...] = value


def sum_grads(grads, n, lanes):
    unused, micro, rows, width = grads.shape
    cols = width // n
    half = n // 2
    dma = pltpu.SemaphoreType.DMA
    piece = pltpu.VMEM((half, rows, cols), bf16)
    small = max(half - 1, 1)
    other = pltpu.VMEM((small, rows, cols), bf16)
    return pl.pallas_call(
        functools.partial(grads_kernel, n, lanes),
        out_shape=(jax.ShapeDtypeStruct((rows, cols), bf16), jax.ShapeDtypeStruct((8, 128), f32)),
        in_specs=[pl.BlockSpec(memory_space=pl.ANY)],
        out_specs=(pl.BlockSpec(memory_space=pltpu.VMEM), pl.BlockSpec(memory_space=pltpu.VMEM)),
        scratch_shapes=[
            pltpu.VMEM((n, micro, rows, cols), bf16), piece, piece, other, other,
            pltpu.VMEM((8, 128), f32), pltpu.VMEM((n - 1, 8, 128), f32),
            pltpu.VMEM((8, 128), f32), pltpu.VMEM((max(lanes - 1, 1), 8, 128), f32),
            dma((n,)), dma((half,)), dma((half,)), dma((small,)), dma((small,)),
            dma((n - 1,)), dma((n - 1,)), dma((max(lanes - 1, 1),)), dma((max(lanes - 1, 1),)),
        ],
        compiler_params=pltpu.CompilerParams(collective_id=0, has_side_effects=True, vmem_limit_bytes=VMEM_BYTES),
    )(grads)


def outer_kernel(n, total, outer, out1, in1, out2, in2, s1, r1, s2, r2):
    half = n // 2
    strip = outer.shape[0]
    greet(n, 1)

    def local(chunk):
        at = pl.ds(pl.multiple_of(chunk * strip, strip), strip)
        return lax.dot_general(total[at, :], total[...], (((1,), (1,)), ((), ())), preferred_element_type=f32)

    def produce(chunk, slot, add, out):
        value = local(chunk)
        if add is not None:
            value = value + add[...].astype(f32)
        out[...] = value.astype(bf16)

    def finish(chunk, slot, add, others):
        value = local(chunk) + add[...].astype(f32)
        for k in range(half - 1):
            value = value + others[k].astype(f32)
        outer[...] = value

    exchange(n, produce, finish, out1, in1, out2, in2, s1, r1, s2, r2)


def sum_outer(total, n):
    rows = total.shape[0]
    strip = rows // n
    half = n // 2
    small = max(half - 1, 1)
    dma = pltpu.SemaphoreType.DMA
    piece = pltpu.VMEM((half, strip, rows), bf16)
    other = pltpu.VMEM((small, strip, rows), bf16)
    return pl.pallas_call(
        functools.partial(outer_kernel, n),
        out_shape=jax.ShapeDtypeStruct((strip, rows), f32),
        in_specs=[pl.BlockSpec(memory_space=pltpu.VMEM)],
        out_specs=pl.BlockSpec(memory_space=pltpu.VMEM),
        scratch_shapes=[piece, piece, other, other, dma((half,)), dma((half,)), dma((small,)), dma((small,))],
        compiler_params=pltpu.CompilerParams(collective_id=1, has_side_effects=True, vmem_limit_bytes=VMEM_BYTES),
    )(total)


def gather_kernel(n, own, every, s1, r1, s2, r2):
    half = n // 2
    me = lax.axis_index("fsdp")
    side = lax.rem(me, 2)
    pair = me // 2
    mate = me + 1 - 2 * side
    greet(n, 1)
    across = [remote(own, every.at[me], s2.at[k], r2.at[k], 2 * lax.rem(pair + 1 + k, half) + side)
              for k in range(half - 1)]
    for copy in across:
        copy.start()
    near = [remote(own, every.at[me], s1.at[0], r1.at[0], mate)]
    near[0].start()
    every[me] = own[...]
    for k in range(half - 1):
        across[k].wait_recv()
        source = 2 * lax.rem(pair + half - 1 - k, half) + side
        near.append(remote(every.at[source], every.at[source], s1.at[k + 1], r1.at[k + 1], mate))
        near[-1].start()
    for copy in near:
        copy.wait()
    for copy in across:
        copy.wait_send()


def gather_rows(own, n, key):
    strip, width = own.shape
    half = n // 2
    small = max(half - 1, 1)
    dma = pltpu.SemaphoreType.DMA
    every = pl.pallas_call(
        functools.partial(gather_kernel, n),
        out_shape=jax.ShapeDtypeStruct((n, strip, width), own.dtype),
        in_specs=[pl.BlockSpec(memory_space=pltpu.VMEM)],
        out_specs=pl.BlockSpec(memory_space=pltpu.VMEM),
        scratch_shapes=[dma((half,)), dma((half,)), dma((small,)), dma((small,))],
        compiler_params=pltpu.CompilerParams(collective_id=key, has_side_effects=True, vmem_limit_bytes=VMEM_BYTES),
    )(own)
    return every.reshape(n * strip, width)


def plain_grads(grads, n, lanes):
    rows = grads.shape[2]
    local = jnp.sum(grads.astype(f32), axis=(0, 1)).astype(bf16)
    pieces = lax.all_to_all(local, "fsdp", split_axis=1, concat_axis=0, tiled=True)
    summed = jnp.sum(pieces.reshape(n, rows, -1).astype(f32), axis=0)
    squares = lax.psum(jnp.sum(summed * summed), ("fsdp", "tp"))
    return summed.astype(bf16), squares


def body(n, lanes, grads, master, moment, second, stats, basis):
    rows, cols = master.shape
    own_rows = basis[0]
    stat_rows = stats[0]
    whole = lax.all_gather(own_rows.astype(bf16), "fsdp", axis=0, tiled=True)
    if cols % 128 == 0 and n % 2 == 0:
        total, squares = sum_grads(grads, n, lanes)
    else:
        total, squares = plain_grads(grads, n, lanes)
    ratio = jnp.minimum(1.0, jnp.sqrt(float(D * KVW) / (jnp.sum(squares) + 1e-06)))
    rotated = mm(whole.T, total) * ratio
    moment_new = 0.9 * moment + 0.1 * rotated
    second_new = 0.95 * second + 0.05 * rotated * rotated
    update = moment_new / (jnp.sqrt(second_new) + 1e-08)
    delta = mm(whole, update)
    master_new = master - 0.01 * (delta + 0.1 * master)
    weights = lax.all_gather(master_new.astype(bf16), "fsdp", axis=1, tiled=True)
    outer = sum_outer(total, n) * (ratio * ratio)
    stats_new = 0.9 * stat_rows + 0.1 / KVW * outer
    top = stats_new.astype(bf16)
    power = mm(top, whole) + mm(stats_new - top.astype(f32), whole)
    every = gather_rows(power.astype(bf16), n, 2)
    raw = mm(every.T, every)
    norm = 1.0 / jnp.sqrt(jnp.sum(jnp.square(every.astype(f32))) + 1e-06)
    gram = raw * (norm * norm)
    current = power * norm
    bend = poly_second * gram + poly_third * mm(gram, gram)
    current = poly_first * current + mm(current, bend)
    once = poly_first * gram + mm(bend, gram)
    gram = poly_first * once + mm(bend, once)
    product = mm(current, gram)
    current = poly_first * current + poly_second * product + poly_third * mm(product, gram)
    return (weights, master_new, moment_new, second_new, stats_new[None], current[None])


def solution(mesh):
    in_specs = (
        P("fsdp", None, "tp", None),
        P("tp", "fsdp"),
        P("tp", "fsdp"),
        P("tp", "fsdp"),
        P("tp", "fsdp", None),
        P("tp", "fsdp", None),
    )
    out_specs = (
        P("tp", None),
        P("tp", "fsdp"),
        P("tp", "fsdp"),
        P("tp", "fsdp"),
        P("tp", "fsdp", None),
        P("tp", "fsdp", None),
    )
    step = functools.partial(body, mesh.shape["fsdp"], mesh.shape["tp"])
    return jax.shard_map(step, mesh=mesh, in_specs=in_specs, out_specs=out_specs, check_vma=False)
```

time: 638 us -> 252 us (0.39)
  waiting for transfers between devices: 484 us -> 0.06 us
  Pallas kernels: 0 us -> 204 us
  blocking collectives: 60.1 us -> 0 us
  matrix products: 43.4 us -> 18.7 us
  local copies, waits for them, and re-layouts: 18.1 us -> 8.19 us
  other arithmetic: 12.6 us -> 5.19 us
    reduce_scatter x2 -> x0, waiting for transfers between devices: 219 us -> none  [the longest x1 148 us: body(): summed = lax.psum_scatter(local, 'fsdp', scatter_dimension=1, tiled=True)]
    pallas_call x0 -> x3, Pallas kernels: none -> 204 us  [the longest x1 90.8 us: sum_grads(): pl.pallas_call(functools.partial(grads_kernel, n, lanes), out_shape=(jax....]
    psum x2 -> x0, waiting for transfers between devices: 182 us -> none  [gram_of(): return lax.psum(local_gram.astype(jnp.bfloat16), 'fsdp').astype(jnp.float32)]
    all_gather x2, waiting for transfers between devices: 82.4 us -> 0.02 us  [the longest x1 0.02 us: body(): whole = lax.all_gather(own_rows.astype(bf16), 'fsdp', axis=0, tiled=True)]
    psum x2 -> x0, blocking collectives: 60.1 us -> none  [the longest x1 42.2 us: body(): squares = lax.psum(jnp.sum(summed * summed), ('fsdp', 'tp'))]
    dot_general x10 -> x11, matrix products: 43.4 us -> 18.7 us  [mm(): return jnp.dot(a.astype(bf16), b.astype(bf16), preferred_element_type=f32)]
    unnamed x27 -> x13, local copies, waits for them, and re-layouts: 18.1 us -> 8.19 us
    reduce_sum x2, other arithmetic: 11.7 us -> 2.28 us  [the longest x1 1.68 us: body(): norm = 1.0 / jnp.sqrt(jnp.sum(jnp.square(every.astype(f32))) + 1e-06)]
  transfers between devices with their start and end apart: 6 -> 2, of which waited for: 6 -> 0; matrix products, arithmetic and copies ran while one was open for 8% -> 7% of each run, Pallas kernels for 0% -> 81%
where the time goes in v2:
time: 252 us
  Pallas kernels  204 us (81%)
  matrix products  18.7 us (7%)
  between operations  15.6 us (6%)
  local copies, waits for them, and re-layouts  8.19 us (3%)
  other arithmetic  5.19 us (2%)
    pallas_call x1, Pallas kernels, sum_grads(): pl.pallas_call(functools.partial(grads_kernel, n, lanes), out_shape=(jax....  90.8 us
    pallas_call x1, Pallas kernels, gather_rows(): pl.pallas_call(functools.partial(gather_kernel, n), out_shape=jax.ShapeDt...  62.3 us
    pallas_call x1, Pallas kernels, sum_outer(): pl.pallas_call(functools.partial(outer_kernel, n), out_shape=jax.ShapeDty...  50.9 us
    dot_general x11, matrix products, mm(): return jnp.dot(a.astype(bf16), b.astype(bf16), preferred_element_type=f32)  18.7 us
    unnamed x13, local copies, waits for them, and re-layouts  8.19 us
  transfers between devices with their start and end apart: 2, of which 0 were waited for; matrix products, arithmetic and copies ran while one was open for 7% of the time, Pallas kernels for 81%

profile of v2, /device:TPU:28, one launch (start us, length us, event | category | flops | bytes accessed | tf_op | source)
XLA Modules:
  0.0 251.8 jit_solution(10031255959244580795)
XLA Ops:
  7.2 0.0 all-gather.6.cloned.1.call-start
  7.2 1.8 convert_element_type.54
  9.0 0.0 all-gather.6.cloned.1.call-update
  9.0 0.0 all-gather.4.cloned.1.call-start
  9.1 0.0 copy-start
  9.1 3.4 %copy-done = bf16[1,2,1024,2048]{3,2,1,0:T(8,128)(2,1)S(1)} copy-done((bf16[1,2,1024,2048]{3,2,1,0:T(8,128)(2,1)S(1)}, bf16[1,2,1024,2048]{3,2,1,0:T(8,128)(2,1)}, u32[]{:S(2)}) %copy-start) | copy-done | bytes 8388632
  12.5 90.8 %shard_map.109 = (bf16[1024,256]{1,0:T(8,128)(2,1)S(1)}, f32[8,128]{1,0:T(8,128)S(1)}) custom-call(bf16[1,2,1024,2048]{3,2,1,0:T(8,128)(2,1)S(1)} %copy-done), custom_call_target="tpu_custom_call" | custom-call | tf_op jit(solution)/shard_map/pallas_call | solution.py:163
  103.3 0.6 reduce_sum.18
  104.6 0.0 all-gather.6.cloned.1.call-done
  104.6 0.0 copy-start.1
  104.7 0.0 copy-start.5
  104.7 3.2 %fusion.38 = (f32[1024,256]{1,0:T(8,128)S(1)}, f32[1024,256]{1,0:T(8,128)S(1)}) fusion(f32[1024,256]{1,0:T(8,128)} %param.9, f32[1024,256]{1,0:T(8,128)} %param.8, f32[]{:T(128)S(6)} %min.3, bf16[1024,256]{1,0:T(8,128)(2,1)S(1)} %get-tuple-element.8.total, bf16[1,1024,1024]{2,1,0:T(8,128)(2,1)} %all-gather.6.cloned.1.call-done), kind=kOutput, calls=%fused_computation.30 | convolution fusion | flops 538968064 | bytes 6815748 | tf_op jit(solution)/shard_map/dot_general | solution.py:23
  107.8 0.0 copy-start.3
  107.9 0.0 copy-start.4
  107.9 0.0 copy-done.1
  107.9 0.0 copy-done.5
  107.9 2.1 fusion.48
  110.0 0.0 copy-done.3
  110.0 0.0 copy-done.4
  110.0 0.0 all-gather.4.cloned.1.call-update
  110.0 50.9 %shard_map.110 = f32[128,1024]{1,0:T(8,128)S(1)} custom-call(bf16[1024,256]{1,0:T(8,128)(2,1)S(1)} %get-tuple-element.8.total), custom_call_target="tpu_custom_call" | custom-call | tf_op jit(solution)/shard_map/pallas_call | solution.py:211
  160.9 1.1 bitcast_add_fusion
  162.0 0.0 copy-start.2
  162.0 0.4 fusion.1
  162.5 0.4 fusion.49
  162.9 0.0 copy-done.2
  163.0 62.3 %shard_map.111 = bf16[8,128,1024]{2,1,0:T(8,128)(2,1)S(1)} custom-call(bf16[128,1024]{1,0:T(8,128)(2,1)S(1)} %get-tuple-element.14.own), custom_call_target="tpu_custom_call" | custom-call | tf_op jit(solution)/shard_map/pallas_call | solution.py:251
  225.3 1.7 multiply_reduce_fusion
  227.6 2.4 fusion.50
  230.1 2.6 %add_convert_fusion.1 = bf16[1024,1024]{1,0:T(8,128)(2,1)S(1)} fusion(f32[1024,1024,1]{1,0,2:T(8,128)S(1)} %fusion.50, f32[]{:T(128)S(6)} %mul.138), kind=kOutput, calls=%fused_computation.3 | convolution fusion | flops 2154823680 | bytes 6291460 | tf_op jit(solution)/shard_map/dot_general | solution.py:23
  232.6 0.5 convolution_add_fusion
  233.1 2.3 fusion.15
  235.5 2.9 %add_convert_fusion = bf16[1024,1024]{1,0:T(8,128)(2,1)S(1)} fusion(bf16[1024,1024]{1,0:T(8,128)(2,1)S(1)} %add_convert_fusion.1, f32[1024,1024]{1,0:T(8,128)S(1)} %fusion.15, f32[1024,1024,1]{1,0,2:T(8,128)S(1)} %fusion.50, f32[]{:T(128)S(6)} %mul.138), kind=kOutput, calls=%fused_computation.1 | convolution fusion | flops 2157969408 | bytes 12582916 | tf_op jit(solution)/shard_map/dot_general | solution.py:23
  238.4 0.4 fusion.41
  238.8 1.3 fusion.37
  240.2 0.0 all-gather.4.cloned.1.call-done
  240.2 4.8 %copy.17 = bf16[1024,2048]{1,0:T(8,128)(2,1)} copy(bf16[1024,2048]{1,0:T(8,128)(2,1)} %all-gather.4.cloned.1.call-done) | data formatting | bytes 8388608
Async XLA Ops:
  7.2 97.5 %all-gather.6.cloned.1.call-start = ((), (), s32[]{:S(2)}) async-start(), calls=%async_computation.1 | async-start | bytes 2359296 | tf_op jit(solution)/shard_map/all_gather | solution.py:275
  9.0 231.2 %all-gather.4.cloned.1.call-start = ((), (), s32[]{:S(2)}) async-start(), calls=%async_computation | async-start | bytes 4718592 | tf_op jit(solution)/shard_map/all_gather | solution.py:287
  9.1 3.4 %copy-start = (bf16[1,2,1024,2048]{3,2,1,0:T(8,128)(2,1)S(1)}, bf16[1,2,1024,2048]{3,2,1,0:T(8,128)(2,1)}, u32[]{:S(2)}) copy-start(bf16[1,2,1024,2048]{3,2,1,0:T(8,128)(2,1)} %grads.1) | copy-start | bytes 25165828
  104.6 3.2 %copy-start.1 = (bf16[1,1024,1024]{2,1,0:T(8,128)(2,1)S(1)}, bf16[1,1024,1024]{2,1,0:T(8,128)(2,1)}, u32[]{:S(2)}) copy-start(bf16[1,1024,1024]{2,1,0:T(8,128)(2,1)} %all-gather.6.cloned.1.call-done) | copy-start | bytes 6291460
  104.7 3.2 %copy-start.5 = (f32[1024,256]{1,0:T(8,128)S(1)}, f32[1024,256]{1,0:T(8,128)}, u32[]{:S(2)}) copy-start(f32[1024,256]{1,0:T(8,128)} %param.7) | copy-start | bytes 3145732
  107.8 2.1 copy-start.3
  107.9 2.1 copy-start.4
  162.0 0.9 copy-start.2
Sparse Core Ops, SparseCore 0:
  10.7 79.4 all-gather.5
  110.1 112.8 all-gather.3

commit v3 on v2

--- a/solution.py
+++ b/solution.py
@@ -42,7 +42,7 @@
     )
 
 
-def exchange(n, produce, finish, out1, in1, out2, in2, s1, r1, s2, r2):
+def exchange(n, produce, finish, out1, in1, out2, in2, s1, r1, s2, r2, beside=None):
     half = n // 2
     me = lax.axis_index("fsdp")
     side = lax.rem(me, 2)
@@ -65,6 +65,8 @@
         if k < half - 1:
             produce(2 * groups[k] + side, 2 * k + 1, in1.at[k], out2.at[k])
             second[k].start()
+        if beside is not None:
+            beside(k)
     for k in range(half - 1):
         second[k].wait_recv()
     finish(me, 2 * half - 1, in1.at[half - 1], in2)
@@ -74,10 +76,11 @@
         second[k].wait_send()
 
 
-def grads_kernel(n, lanes, grads, total, squares, held, out1, in1, out2, in2, own_sq, in_sq, lane_sq, in_lane,
-                 loads, s1, r1, s2, r2, sq_s, sq_r, lane_s, lane_r):
+def grads_kernel(n, lanes, grads, basis, total, squares, whole, held, out1, in1, out2, in2, own_sq, in_sq, lane_sq, in_lane,
+                 loads, s1, r1, s2, r2, sq_s, sq_r, lane_s, lane_r, b1, c1, b2, c2):
     half = n // 2
     rows, cols = total.shape
+    strip = basis.shape[0]
     micro = held.shape[1]
     tile = 128
     me = lax.axis_index("fsdp")
@@ -132,7 +135,26 @@
             part = part + sums[:, c * 128 : (c + 1) * 128]
         own_sq[...] = part
 
-    exchange(n, produce, finish, out1, in1, out2, in2, s1, r1, s2, r2)
+    mate = me + 1 - 2 * side
+    here = pl.ds(pl.multiple_of(me * strip, strip), strip)
+    across = [remote(basis, whole.at[here], b2.at[k], c2.at[k], 2 * lax.rem(pair + 1 + k, half) + side)
+              for k in range(half - 1)]
+    near = []
+
+    def beside(k):
+        if k == 0:
+            for copy in across:
+                copy.start()
+            near.append(remote(basis, whole.at[here], b1.at[0], c1.at[0], mate))
+            whole[here, :] = basis[...]
+        else:
+            across[k - 1].wait_recv()
+            source = 2 * lax.rem(pair + half - k, half) + side
+            there = pl.ds(pl.multiple_of(source * strip, strip), strip)
+            near.append(remote(whole.at[there], whole.at[there], b1.at[k], c1.at[k], mate))
+        near[-1].start()
+
+    exchange(n, produce, finish, out1, in1, out2, in2, s1, r1, s2, r2, beside)
     sends = [remote(own_sq, in_sq.at[k], sq_s.at[k], sq_r.at[k], lax.rem(me + 1 + k, n)) for k in range(n - 1)]
     for send in sends:
         send.start()
@@ -150,9 +172,13 @@
         send.wait()
         value = value + in_lane[k]
     squares[...] = value
-
-
-def sum_grads(grads, n, lanes):
+    for copy in near:
+        copy.wait()
+    for copy in across:
+        copy.wait_send()
+
+
+def sum_grads(grads, basis, n, lanes):
     unused, micro, rows, width = grads.shape
     cols = width // n
     half = n // 2
@@ -162,18 +188,20 @@
     other = pltpu.VMEM((small, rows, cols), bf16)
     return pl.pallas_call(
         functools.partial(grads_kernel, n, lanes),
-        out_shape=(jax.ShapeDtypeStruct((rows, cols), bf16), jax.ShapeDtypeStruct((8, 128), f32)),
-        in_specs=[pl.BlockSpec(memory_space=pl.ANY)],
-        out_specs=(pl.BlockSpec(memory_space=pltpu.VMEM), pl.BlockSpec(memory_space=pltpu.VMEM)),
+        out_shape=(jax.ShapeDtypeStruct((rows, cols), bf16), jax.ShapeDtypeStruct((8, 128), f32),
+                   jax.ShapeDtypeStruct((n * basis.shape[0], basis.shape[1]), bf16)),
+        in_specs=[pl.BlockSpec(memory_space=pl.ANY), pl.BlockSpec(memory_space=pltpu.VMEM)],
+        out_specs=(pl.BlockSpec(memory_space=pltpu.VMEM),) * 3,
         scratch_shapes=[
             pltpu.VMEM((n, micro, rows, cols), bf16), piece, piece, other, other,
             pltpu.VMEM((8, 128), f32), pltpu.VMEM((n - 1, 8, 128), f32),
             pltpu.VMEM((8, 128), f32), pltpu.VMEM((max(lanes - 1, 1), 8, 128), f32),
             dma((n,)), dma((half,)), dma((half,)), dma((small,)), dma((small,)),
             dma((n - 1,)), dma((n - 1,)), dma((max(lanes - 1, 1),)), dma((max(lanes - 1, 1),)),
+            dma((half,)), dma((half,)), dma((small,)), dma((small,)),
         ],
-        compiler_params=pltpu.CompilerParams(collective_id=0, has_side_effects=True, vmem_limit_bytes=VMEM_BYTES),
-    )(grads)
+        compiler_params=pltpu.CompilerParams(collective_id=0, has_side_effects=True, vmem_limit_bytes=57 * 1024 * 1024),
+    )(grads, basis)
 
 
 def outer_kernel(n, total, outer, out1, in1, out2, in2, s1, r1, s2, r2):
@@ -259,6 +287,138 @@
     return every.reshape(n * strip, width)
 
 
+SLICES = 4
+
+
+def tail_kernel(n, power, own, weights, refreshed, every, gram, gram_low, bend, once, local,
+                s1, r1, s2, r2, u1, v1, u2, v2):
+    half = n // 2
+    strip = power.shape[0]
+    rows, cols = own.shape
+    part = rows // SLICES
+    block = 512
+    me = lax.axis_index("fsdp")
+    side = lax.rem(me, 2)
+    pair = me // 2
+    mate = me + 1 - 2 * side
+    greet(n, 1)
+    here = pl.ds(pl.multiple_of(me * strip, strip), strip)
+    every[here, :] = power[...].astype(bf16)
+    targets = [2 * lax.rem(pair + 1 + k, half) + side for k in range(half - 1)]
+    sources = [2 * lax.rem(pair + half - 1 - k, half) + side for k in range(half - 1)]
+    across = [remote(every.at[here], every.at[here], s2.at[k], r2.at[k], targets[k]) for k in range(half - 1)]
+    near = [remote(every.at[here], every.at[here], s1.at[0], r1.at[0], mate)]
+    for copy in across + near:
+        copy.start()
+
+    def window(device, piece):
+        return weights.at[pl.ds(piece * part, part), pl.ds(pl.multiple_of(device * cols, 128), cols)]
+
+    mine = pltpu.make_async_copy(own, weights.at[:, pl.ds(pl.multiple_of(me * cols, 128), cols)], local.at[0])
+    mine.start()
+    wide = []
+    close = []
+
+    def push(piece):
+        for k in range(half - 1):
+            wide.append(remote(own.at[pl.ds(piece * part, part)], window(me, piece),
+                               u2.at[piece, k], v2.at[piece, k], targets[k]))
+            wide[-1].start()
+        close.append(remote(own.at[pl.ds(piece * part, part)], window(me, piece),
+                            u1.at[piece, half - 1], v1.at[piece, half - 1], mate))
+        close[-1].start()
+
+    def relay(piece):
+        for k in range(half - 1):
+            wide[piece * (half - 1) + k].wait_recv()
+            close.append(remote(window(sources[k], piece), window(sources[k], piece),
+                                u1.at[piece, k], v1.at[piece, k], mate))
+            close[-1].start()
+
+    for k in range(half - 1):
+        across[k].wait_recv()
+        there = pl.ds(pl.multiple_of(sources[k] * strip, strip), strip)
+        near.append(remote(every.at[there], every.at[there], s1.at[k + 1], r1.at[k + 1], mate))
+        near[-1].start()
+    push(0)
+    push(1)
+    for copy in near:
+        copy.wait_recv()
+
+    def sums(i, carry):
+        value = every[pl.ds(pl.multiple_of(i * 128, 128), 128), :].astype(f32)
+        return carry + jnp.sum((value * value).reshape(16, 8, rows), axis=0)
+
+    total_sq = jnp.sum(lax.fori_loop(0, rows // 128, sums, jnp.zeros((8, rows), f32)), keepdims=True)
+    norm = 1.0 / jnp.sqrt(total_sq + 1e-06)
+
+    def blocks(step):
+        def run(i, carry):
+            step(pl.ds(pl.multiple_of(i * block, block), block))
+            return carry
+
+        lax.fori_loop(0, rows // block, run, 0)
+
+    def make_gram(at):
+        value = lax.dot_general(every[:, at], every[...], (((0,), (0,)), ((), ())), preferred_element_type=f32)
+        value = value * (norm * norm)
+        gram[at, :] = value
+        gram_low[at, :] = value.astype(bf16)
+
+    def make_bend(at):
+        value = poly_second * gram[at, :] + poly_third * mm(gram_low[at, :], gram_low[...])
+        bend[at, :] = value.astype(bf16)
+
+    def make_once(at):
+        value = poly_first * gram[at, :] + mm(bend[at, :], gram_low[...])
+        gram[at, :] = value
+        once[at, :] = value.astype(bf16)
+
+    def make_second(at):
+        value = poly_first * gram[at, :] + mm(bend[at, :], once[...])
+        gram_low[at, :] = value.astype(bf16)
+
+    blocks(make_gram)
+    blocks(make_bend)
+    relay(0)
+    if SLICES > 2:
+        push(2)
+    blocks(make_once)
+    blocks(make_second)
+    current = power[...] * norm
+    current = poly_first * current + mm(current, bend[...])
+    product = mm(current, gram_low[...])
+    refreshed[...] = poly_first * current + poly_second * product + poly_third * mm(product, gram_low[...])
+    for piece in range(1, SLICES):
+        relay(piece)
+        if piece + 2 < SLICES:
+            push(piece + 2)
+    mine.wait()
+    for copy in close:
+        copy.wait()
+    for copy in wide + near + across:
+        copy.wait_send()
+
+
+def finish_step(power, own, n):
+    strip, width = power.shape
+    rows, cols = own.shape
+    half = n // 2
+    small = max(half - 1, 1)
+    dma = pltpu.SemaphoreType.DMA
+    low = pltpu.VMEM((width, width), bf16)
+    return pl.pallas_call(
+        functools.partial(tail_kernel, n),
+        out_shape=(jax.ShapeDtypeStruct((rows, n * cols), bf16), jax.ShapeDtypeStruct((strip, width), f32)),
+        in_specs=[pl.BlockSpec(memory_space=pltpu.VMEM)] * 2,
+        out_specs=(pl.BlockSpec(memory_space=pl.ANY), pl.BlockSpec(memory_space=pltpu.VMEM)),
+        scratch_shapes=[low, pltpu.VMEM((width, width), f32), low, low, low, dma((1,)),
+                        dma((half,)), dma((half,)), dma((small,)), dma((small,)),
+                        dma((SLICES, half)), dma((SLICES, half)), dma((SLICES, small)), dma((SLICES, small))],
+        compiler_params=pltpu.CompilerParams(collective_id=3, has_side_effects=True, vmem_limit_bytes=VMEM_BYTES),
+    )(power, own)
+
+
 def plain_grads(grads, n, lanes):
     rows = grads.shape[2]
     local = jnp.sum(grads.astype(f32), axis=(0, 1)).astype(bf16)
@@ -272,10 +432,11 @@
     rows, cols = master.shape
     own_rows = basis[0]
     stat_rows = stats[0]
-    whole = lax.all_gather(own_rows.astype(bf16), "fsdp", axis=0, tiled=True)
-    if cols % 128 == 0 and n % 2 == 0:
-        total, squares = sum_grads(grads, n, lanes)
+    aligned = cols % 128 == 0 and n % 2 == 0
+    if aligned:
+        total, squares, whole = sum_grads(grads, own_rows.astype(bf16), n, lanes)
     else:
+        whole = lax.all_gather(own_rows.astype(bf16), "fsdp", axis=0, tiled=True)
         total, squares = plain_grads(grads, n, lanes)
     ratio = jnp.minimum(1.0, jnp.sqrt(float(D * KVW) / (jnp.sum(squares) + 1e-06)))
     rotated = mm(whole.T, total) * ratio
@@ -284,11 +445,14 @@
     update = moment_new / (jnp.sqrt(second_new) + 1e-08)
     delta = mm(whole, update)
     master_new = master - 0.01 * (delta + 0.1 * master)
-    weights = lax.all_gather(master_new.astype(bf16), "fsdp", axis=1, tiled=True)
     outer = sum_outer(total, n) * (ratio * ratio)
     stats_new = 0.9 * stat_rows + 0.1 / KVW * outer
     top = stats_new.astype(bf16)
     power = mm(top, whole) + mm(stats_new - top.astype(f32), whole)
+    if aligned:
+        weights, current = finish_step(power, master_new.astype(bf16), n)
+        return (weights, master_new, moment_new, second_new, stats_new[None], current[None])
+    weights = lax.all_gather(master_new.astype(bf16), "fsdp", axis=1, tiled=True)
     every = gather_rows(power.astype(bf16), n, 2)
     raw = mm(every.T, every)
     norm = 1.0 / jnp.sqrt(jnp.sum(jnp.square(every.astype(f32))) + 1e-06)

time: 252 us -> 231 us (0.917)
  matrix products: 18.7 us -> 3.6 us
  between operations: 15.6 us -> 1.5 us
  Pallas kernels: 204 us -> 216 us
  local copies, waits for them, and re-layouts: 8.19 us -> 5.28 us
    pallas_call x1, Pallas kernels: 62.3 us -> 87.7 us  [finish_step(): pl.pallas_call(functools.partial(tail_kernel, n), out_shape=(jax.ShapeDty...]
    pallas_call x1, Pallas kernels: 50.9 us -> 35.7 us  [sum_outer(): pl.pallas_call(functools.partial(outer_kernel, n), out_shape=jax.ShapeDty...]
    dot_general x11 -> x4, matrix products: 18.7 us -> 3.6 us  [mm(): return jnp.dot(a.astype(bf16), b.astype(bf16), preferred_element_type=f32)]
    unnamed x13 -> x20, local copies, waits for them, and re-layouts: 8.19 us -> 5.28 us
  transfers between devices with their start and end apart: 2 -> 0, of which waited for: 0 -> 0; matrix products, arithmetic and copies ran while one was open for 7% -> 0% of each run, Pallas kernels for 81% -> 0%
where the time goes in v3:
time: 231 us; the launch traced here: 230 us
  Pallas kernels  216 us (94%)
  local copies, waits for them, and re-layouts  5.28 us (2%)
  matrix products  3.6 us (2%)
  other arithmetic  3.16 us (1%)
    pallas_call x1, Pallas kernels, sum_grads(): pl.pallas_call(functools.partial(grads_kernel, n, lanes), out_shape=(jax....  93 us
    pallas_call x1, Pallas kernels, finish_step(): pl.pallas_call(functools.partial(tail_kernel, n), out_shape=(jax.ShapeDty...  87.7 us
    pallas_call x1, Pallas kernels, sum_outer(): pl.pallas_call(functools.partial(outer_kernel, n), out_shape=jax.ShapeDty...  35.7 us
    unnamed x20, local copies, waits for them, and re-layouts  5.28 us

profile of v3, /device:TPU:28, one launch (start us, length us, event | category | flops | bytes accessed | tf_op | source)
XLA Modules:
  0.0 229.9 jit_solution(7624672382019663081)
XLA Ops:
  0.6 1.8 convert_bitcast_fusion.basis
  2.4 0.0 copy-start.7
  2.4 93.0 %shard_map.109 = (bf16[1024,256]{1,0:T(8,128)(2,1)}, f32[8,128]{1,0:T(8,128)}, bf16[1024,1024]{1,0:T(8,128)(2,1)}) custom-call(bf16[1,2,1024,2048]{3,2,1,0:T(8,128)(2,1)} %grads.1, bf16[128,1024]{1,0:T(8,128)(2,1)} %convert_bitcast_fusion.basis), custom_call_target="tpu_custom_call" | custom-call | tf_op jit(solution)/shard_map/pallas_call | solution.py:189
  95.4 1.3 reduce_sum.9
  97.4 0.0 copy-start
  97.5 1.0 copy-done
  98.5 0.0 copy-start.1
  98.5 35.7 %shard_map.110 = f32[128,1024]{1,0:T(8,128)S(1)} custom-call(bf16[1024,256]{1,0:T(8,128)(2,1)S(1)} %copy-done), custom_call_target="tpu_custom_call" | custom-call | tf_op jit(solution)/shard_map/pallas_call | solution.py:239
  134.2 0.0 copy-done.7
  134.2 0.1 bitcast_add_fusion
  134.3 0.0 copy-start.2
  134.3 0.0 copy-done.1
  134.3 0.4 fusion.5
  134.8 0.0 copy-start.3
  134.8 0.0 copy-start.4
  134.8 0.4 convolution_add_fusion.1.power
  135.2 0.0 copy-done.2
  135.2 0.7 copy-done.3
  136.0 0.3 copy-done.4
  136.3 0.0 copy-start.8
  136.3 0.8 fusion.2
  137.2 0.0 copy-start.5
  137.2 0.0 copy-start.6
  137.2 0.3 copy-done.8
  137.5 1.9 fusion.8
  139.4 0.0 copy-done.5
  139.4 0.0 copy-done.6
  139.4 87.7 %shard_map.111 = (bf16[1024,2048]{1,0:T(8,128)(2,1)S(1)}, f32[128,1024]{1,0:T(8,128)S(1)}) custom-call(f32[128,1024]{1,0:T(8,128)S(1)} %convolution_add_fusion.1.power, bf16[1024,256]{1,0:T(8,128)(2,1)S(1)} %get-tuple-element.18.own), custom_call_target="tpu_custom_call" | custom-call | tf_op jit(solution)/shard_map/pallas_call | solution.py:410
  227.1 2.0 copy.14
  229.1 0.8 copy.15
Async XLA Ops:
  2.4 131.8 %copy-start.7 = (f32[1,128,1024]{2,1,0:T(8,128)S(1)}, f32[1,128,1024]{2,1,0:T(8,128)}, u32[]{:S(2)}) copy-start(f32[1,128,1024]{2,1,0:T(8,128)} %param.10) | copy-start | bytes 1572868
  97.4 1.0 copy-start
  98.5 35.8 %copy-start.1 = (bf16[1024,1024]{1,0:T(8,128)(2,1)S(1)}, bf16[1024,1024]{1,0:T(8,128)(2,1)}, u32[]{:S(2)}) copy-start(bf16[1024,1024]{1,0:T(8,128)(2,1)} %get-tuple-element.13) | copy-start | bytes 6291460
  134.3 1.0 copy-start.2
  134.8 1.2 copy-start.3
  134.8 1.5 copy-start.4
  136.3 1.2 copy-start.8
  137.2 2.2 copy-start.5
  137.2 2.2 copy-start.6
